TPU v7x, 32 devices: a whole 2x2x4 slice. The times are simulated.
32 devices in a mesh: seq: 8 (over z, x), tp: 4 (over y, core).
Axes of the slice: x: 2, y: 2, z: 4, core: 2. Of those that a mesh axis runs over, the one named last changes fastest.
Arguments:
- hidden_new: bfloat16 [3, 16, 8192], P(None, None, 'seq'), may hold values from -6 to 6
- w_kv: bfloat16 [8192, 8, 256], P('seq', 'tp'), may hold values from -0.0625 to 0.0625
- w_out: bfloat16 [8192, 8192], P('tp', 'seq'), may hold values from -0.0625 to 0.0625
- queries_draft: bfloat16 [3, 4, 8, 32, 128], P(None, None, 'tp'), may hold values from -48 to 48
- queries_verify: bfloat16 [3, 4, 8, 32, 128], P(None, None, 'tp'), may hold values from -48 to 48
- keys_cache: bfloat16 [4, 8, 16384, 128], P(None, 'tp', 'seq'), may hold values from -6 to 6
- values_cache: bfloat16 [4, 8, 16384, 128], P(None, 'tp', 'seq'), may hold values from -6 to 6
- key_levels: bfloat16 [4, 8, 16384, 128], P(None, 'tp', 'seq'), may hold values from -8 to 7, as said below
- value_levels: bfloat16 [4, 8, 16384, 128], P(None, 'tp', 'seq'), may hold values from -8 to 7, as said below
- key_scales: float32 [4, 8, 16384], P(None, 'tp', 'seq'), may hold values from 0.05 to 0.5
- value_scales: float32 [4, 8, 16384], P(None, 'tp', 'seq'), may hold values from 0.1 to 0.4
- lengths: int32 [4], replicated, may hold values from 2 to 16376, as said below
- accepted: int32 [2, 4], replicated, may hold values from 0 to 4, as said below
Outputs:
- layer_out: bfloat16 [3, 2, 16, 8192], P(None, None, None, 'seq')
Inputs may be any that keep to these rules, and one draw needn't show every extreme that they name: `key_levels`: every entry is a whole number. Positions 0 and 1 of every sequence and head hold equal levels. `value_levels`: every entry is a whole number. `lengths`: some sequence starts with exactly 16376 valid positions, another with 16 or fewer. `accepted`: the values 0 and 4 both occur.
All inputs are finite; a program needn't handle non-finite values.
Results may differ from a plain program's by a relative error of at most 0.006.
The roundings to bfloat16 on the way count: a program that leaves them out, or rounds other values in their place, can miss the bound.
Values may be sent and summed in bfloat16 or wider, within the bound.
A program may use at most 128 MiB of HBM per device.

v0:
```python
import math
import jax
import jax.numpy as jnp
from jax import lax
from jax.sharding import PartitionSpec as P

HD = 128
GROUP = 8
R = 4
ROUNDS = 3
NEG = -1e30


def dequantize(levels, scales):
    return (levels.astype(jnp.float32) * scales[..., None]).astype(jnp.bfloat16)


def attend(queries, keys, values, usable):
    scores = jnp.einsum("bhqd,bhkd->bhqk", queries, keys, preferred_element_type=jnp.float32) * (
        1.0 / math.sqrt(HD)
    )
    scores = jnp.where(usable, scores, NEG)
    maxima = jnp.max(scores, axis=-1)
    weights = jnp.where(usable, jnp.exp(scores - maxima[..., None]), 0.0).astype(jnp.bfloat16)
    totals = jnp.sum(weights.astype(jnp.float32), axis=-1)
    weighted = jnp.einsum("bhqk,bhkd->bhqd", weights, values, preferred_element_type=jnp.float32)
    return (maxima, totals, weighted)


def combine(former, latter):
    highest = jnp.maximum(former[0], latter[0])
    former_w = jnp.exp(former[0] - highest)
    latter_w = jnp.exp(latter[0] - highest)
    return (
        highest,
        former[1] * former_w + latter[1] * latter_w,
        former[2] * former_w[..., None] + latter[2] * latter_w[..., None],
    )


def finish(partial_value):
    return (partial_value[2] / partial_value[1][..., None]).astype(jnp.bfloat16)


def arrange(attended):
    kind_count, batch_size, head_count, query_rows, head_width = attended.shape
    split_rows = attended.reshape(kind_count, batch_size, head_count, GROUP, R, head_width)
    return split_rows.transpose(0, 1, 4, 2, 3, 5).reshape(
        kind_count * batch_size * R, head_count * GROUP * head_width
    )


def stacked_rows(draft_part, verify_part):
    maxima = jnp.stack([draft_part[0], verify_part[0]]).reshape(1, -1)
    totals = jnp.stack([draft_part[1], verify_part[1]]).reshape(1, -1)
    weighted = jnp.stack([draft_part[2], verify_part[2]]).reshape(1, maxima.shape[1], -1)
    return (maxima, totals, weighted)


def spread_merge(draft_part, verify_part, draft_self, verify_self, seq_index):
    maxima, totals, weighted = stacked_rows(draft_part, verify_part)
    maxima, totals, weighted = (
        lax.all_to_all(maxima, "seq", split_axis=1, concat_axis=0, tiled=True),
        lax.all_to_all(totals, "seq", split_axis=1, concat_axis=0, tiled=True),
        lax.all_to_all(weighted, "seq", split_axis=1, concat_axis=0, tiled=True),
    )
    highest = jnp.max(maxima, axis=0)
    factors = jnp.exp(maxima - highest[None])
    share_part = (
        highest,
        jnp.sum(totals * factors, axis=0),
        jnp.sum(weighted * factors[..., None], axis=0),
    )
    share_rows = highest.shape[0]
    self_max, self_tot, self_sum = stacked_rows(draft_self, verify_self)
    row_start = seq_index * share_rows
    self_share = (
        lax.dynamic_slice_in_dim(self_max[0], row_start, share_rows, 0),
        lax.dynamic_slice_in_dim(self_tot[0], row_start, share_rows, 0),
        lax.dynamic_slice_in_dim(self_sum[0], row_start, share_rows, 0),
    )
    merged = finish(combine(share_part, self_share))
    gathered = lax.all_gather(merged, "seq", axis=0, tiled=True)
    return gathered.reshape((2,) + draft_part[2].shape)


def per_device(
    hidden_new,
    w_kv,
    w_out,
    queries_draft,
    queries_verify,
    keys_cache,
    values_cache,
    key_levels,
    value_levels,
    key_scales,
    value_scales,
    lengths,
    accepted,
):
    batch_size, head_count, local_len, head_width = keys_cache.shape
    seq_index = lax.axis_index("seq")
    first_row = seq_index * local_len
    key_low = dequantize(key_levels, key_scales)
    value_low = dequantize(value_levels, value_scales)
    places = first_row + jnp.arange(local_len, dtype=jnp.int32)
    stored = (places[None, :] < lengths[:, None])[:, None, :, None]
    flat_kv = w_kv.reshape(w_kv.shape[0], -1)
    tokens = jnp.arange(GROUP * R, dtype=jnp.int32) % R
    causal = (tokens[:, None] >= jnp.arange(R, dtype=jnp.int32)[None, :])[None, None]
    offsets = jnp.arange(R, dtype=jnp.int32)[None, :]
    batch_rows = jnp.broadcast_to(jnp.arange(batch_size, dtype=jnp.int32)[:, None], (batch_size, R))
    length_now = lengths
    results = []
    for turn_index in range(ROUNDS):
        partial_kv = jnp.dot(hidden_new[turn_index], flat_kv, preferred_element_type=jnp.float32)
        fresh_rows = (
            lax.psum(partial_kv, "seq")
            .astype(jnp.bfloat16)
            .reshape(batch_size, R, head_count, 2, head_width)
        )
        new_keys = fresh_rows[:, :, :, 0].transpose(0, 2, 1, 3)
        new_values = fresh_rows[:, :, :, 1].transpose(0, 2, 1, 3)
        usable = (places[None, :] < length_now[:, None])[:, None, None, :]
        draft_q = queries_draft[turn_index]
        verify_q = queries_verify[turn_index]
        draft_keys = jnp.where(stored, key_low, keys_cache)
        draft_values = jnp.where(stored, value_low, values_cache)
        draft_part = attend(draft_q, draft_keys, draft_values, usable)
        draft_self = attend(draft_q, new_keys, new_values, causal)
        verify_part = attend(verify_q, keys_cache, values_cache, usable)
        verify_self = attend(verify_q, new_keys, new_values, causal)
        attended = spread_merge(draft_part, verify_part, draft_self, verify_self, seq_index)
        projected = jnp.dot(arrange(attended), w_out, preferred_element_type=jnp.float32)
        summed = lax.psum(projected, "tp")
        results.append(summed.astype(jnp.bfloat16).reshape(2, batch_size * R, -1))
        if turn_index + 1 < ROUNDS:
            accepted_now = accepted[turn_index]
            targets = length_now[:, None] + offsets - first_row
            landing = (offsets < accepted_now[:, None]) & (targets >= 0) & (targets < local_len)
            targets = jnp.where(landing, targets, local_len)
            keys_cache = keys_cache.at[batch_rows, :, targets, :].set(
                fresh_rows[:, :, :, 0], mode="drop"
            )
            values_cache = values_cache.at[batch_rows, :, targets, :].set(
                fresh_rows[:, :, :, 1], mode="drop"
            )
            length_now = length_now + accepted_now
    return jnp.stack(results)


def solution(mesh):
    return jax.shard_map(
        per_device,
        mesh=mesh,
        in_specs=(
            P(None, None, "seq"),
            P("seq", "tp", None),
            P("tp", "seq"),
            P(None, None, "tp", None, None),
            P(None, None, "tp", None, None),
            P(None, "tp", "seq", None),
            P(None, "tp", "seq", None),
            P(None, "tp", "seq", None),
            P(None, "tp", "seq", None),
            P(None, "tp", "seq"),
            P(None, "tp", "seq"),
            P(),
            P(),
        ),
        out_specs=P(None, None, None, "seq"),
        check_vma=False,
    )
```

profile of v0, /device:TPU:0, one launch (start us, length us, event | category | flops | bytes accessed | tf_op | source)
XLA Modules:
  0.0 335.9 jit_solution(9079900889281217494)
XLA Ops:
  0.0 4.6 %copy.174 = bf16[4,2,2048,128]{3,2,1,0:T(8,128)(2,1)} copy(bf16[4,2,2048,128]{3,2,1,0:T(8,128)(2,1)} %param.18) | data formatting | bytes 8388608
  4.6 2.0 copy.175
  6.7 3.9 %fusion.169 = (f32[4,2,32]{2,1,0:T(2,128)S(1)}, f32[4,2,32,2048]{3,2,1,0:T(8,128)S(1)}) fusion(bf16[4,2,2048,128]{3,2,1,0:T(8,128)(2,1)} %copy.174, bf16[3,4,2,32,128]{4,3,2,1,0:T(8,128)(2,1)S(1)} %copy-done.16, pred[4,2048]{1,0:T(4,128)(4,1)S(1)} %get-tuple-element.48), kind=kOutput, calls=%fused_computation.242 | convolution fusion | flops 135790336 | bytes 6366208 | tf_op jit(solution)/shard_map/bhqd,bhkd->bhqk/dot_general | solution.py:19
  10.7 5.9 %fusion.170 = (f32[4,2,32]{2,1,0:T(2,128)S(1)}, f32[4,2,32,2048]{3,2,1,0:T(8,128)S(1)}) fusion(bf16[3,4,2,32,128]{4,3,2,1,0:T(8,128)(2,1)} %param.16, bf16[4,2,2048,128]{3,2,1,0:T(8,128)(2,1)S(1)} %copy-done.2, pred[4,2048]{1,0:T(4,128)(4,1)S(1)} %get-tuple-element.48, f32[4,2,2048]{2,1,0:T(2,128)S(1)} %copy-done.22, bf16[4,2,2048,128]{3,2,1,0:T(8,128)(2,1)} %param.20), kind=kOutput, calls=%fused_computation.243 | convolution fusion | flops 144178944 | bytes 10634240 | tf_op jit(solution)/shard_map/bhqd,bhkd->bhqk/dot_general | solution.py:19
  16.6 0.9 convert_reduce_fusion.5
  17.5 0.4 copy-done.8
  17.9 0.7 all_to_all.104
  18.6 7.3 %all-to-all-start.2 = ((f32[1,8,64]{2,0,1:T(1,128)}), f32[1,8,64]{2,0,1:T(1,128)S(1)}, u32[]{:S(2)}, u32[]{:S(2)}) async-start(f32[1,8,64]{2,0,1:T(1,128)} %all_to_all.104), calls=%async_computation.2 | async-start | bytes 8192 | tf_op jit(solution)/shard_map/all_to_all | solution.py:64
  25.9 0.2 copy.99
  26.1 0.2 fusion.111
  26.4 0.3 fusion.113
  26.6 0.3 fusion.115
  26.9 38.5 %all-reduce = (bf16[16,512]{1,0:T(8,128)(2,1)S(1)}, bf16[16,512]{1,0:T(8,128)(2,1)S(1)}, bf16[16,512]{1,0:T(8,128)(2,1)S(1)}) all-reduce(f32[16,512]{1,0:T(8,128)S(1)} %fusion.111, f32[16,512]{1,0:T(8,128)S(1)} %fusion.115, f32[16,512]{1,0:T(8,128)S(1)} %fusion.113), channel_id=1, replica_groups=mesh['seq'=8,'tp'=4] {'seq'}, use_global_device_ids=true, to_apply=%region_34.35 | all-reduce | flops 24576 | bytes 147456 | tf_op jit(solution)/shard_map/psum | solution.py:119
  66.8 2.5 scatter_fusion
  69.3 10.5 %copy.76 = bf16[4,2,2048,128]{3,1,2,0:T(2,128)(2,1)} copy(bf16[4,2,2048,128]{3,2,1,0:T(8,128)(2,1)} %scatter_fusion) | data formatting | bytes 8388608 | tf_op jit(solution)/shard_map/scatter | solution.py:143
  80.0 2.6 scatter_fusion.2
  82.6 8.5 %fusion.162 = (f32[4,2,32]{2,1,0:T(2,128)S(1)}, f32[4,2,32,2048]{3,2,1,0:T(8,128)}) fusion(bf16[3,4,2,32,128]{4,3,2,1,0:T(8,128)(2,1)S(1)} %copy-done.21, pred[4,2048]{1,0:T(4,128)(4,1)S(1)} %get-tuple-element.48, bf16[4,2,2048,128]{3,1,2,0:T(2,128)(2,1)} %scatter_fusion.2, f32[4,2,2048]{2,1,0:T(2,128)S(1)} %copy-done.23, ...), kind=kOutput, calls=%fused_computation.235 | convolution fusion | flops 144178944 | bytes 10634240 | tf_op jit(solution)/shard_map/bhqd,bhkd->bhqk/dot_general | solution.py:19
  91.1 2.9 fusion.161
  94.0 6.2 %fusion.168 = (f32[4,2,32]{2,1,0:T(2,128)S(1)}, f32[4,2,32,2048]{3,2,1,0:T(8,128)}) fusion(bf16[3,4,2,32,128]{4,3,2,1,0:T(8,128)(2,1)S(1)} %copy-done.21, bf16[4,2,2048,128]{3,2,1,0:T(8,128)(2,1)S(1)} %copy-done.3, pred[4,2048]{1,0:T(4,128)(4,1)S(1)} %get-tuple-element.48, f32[4,2,2048]{2,1,0:T(2,128)S(1)} %copy-done.23, ...), kind=kOutput, calls=%fused_computation.241 | convolution fusion | flops 144178944 | bytes 10634240 | tf_op jit(solution)/shard_map/bhqd,bhkd->bhqk/dot_general | solution.py:19
  100.2 2.8 fusion.167
  103.1 0.9 convolution_bitcast_fusion.1
  104.0 0.6 copy-done.9
  104.7 1.2 copy-done.20
  105.9 4.2 %fusion.66 = f32[1,4,2,32,128]{4,3,2,1,0:T(8,128)S(1)} fusion(bf16[4,2,2048,128]{3,2,1,0:T(8,128)(2,1)S(1)} %copy-done, pred[4,2048]{1,0:T(4,128)(4,1)S(1)} %get-tuple-element.48, f32[4,2,2048]{2,1,0:T(2,128)S(1)} %copy-done.24, bf16[4,2,2048,128]{3,2,1,0:T(8,128)(2,1)S(1)} %copy-done.20, f32[4,2,32,2048]{3,2,1,0:T(8,128)S(1)} %copy-done.9, ...), kind=kOutput, calls=%fused_computation.62 | convolution fusion | flops 144179200 | bytes 10691584 | tf_op jit(solution)/shard_map/bhqk,bhkd->bhqd/dot_general | solution.py:26
  110.2 0.7 pad_maximum_fusion
  110.9 2.5 scatter_fusion.1
  113.4 10.6 %copy.80 = bf16[4,2,2048,128]{3,1,2,0:T(2,128)(2,1)} copy(bf16[4,2,2048,128]{3,2,1,0:T(8,128)(2,1)} %scatter_fusion.1) | data formatting | bytes 8388608 | tf_op jit(solution)/shard_map/scatter | solution.py:146
  124.0 6.0 %fusion.69 = f32[1,4,2,32,128]{4,3,2,1,0:T(8,128)S(1)} fusion(bf16[4,2,2048,128]{3,2,1,0:T(8,128)(2,1)S(1)} %copy-done.1, pred[4,2048]{1,0:T(4,128)(4,1)S(1)} %get-tuple-element.48, f32[4,2,2048]{2,1,0:T(2,128)S(1)} %copy-done.24, bf16[4,2,2048,128]{3,2,1,0:T(8,128)(2,1)} %param.21, f32[4,2,32,2048]{3,2,1,0:T(8,128)S(1)} %copy-done.12, ...), kind=kOutput, calls=%fused_computation.63 | convolution fusion | flops 144179200 | bytes 10699776 | tf_op jit(solution)/shard_map/bhqk,bhkd->bhqd/dot_general | solution.py:26
  130.0 0.9 convolution_bitcast_fusion
  131.0 2.6 scatter_fusion.3
  133.6 7.2 %fusion.72 = f32[1,4,2,32,128]{4,3,2,1,0:T(8,128)S(1)} fusion(pred[4,2048]{1,0:T(4,128)(4,1)S(1)} %get-tuple-element.48, bf16[4,2,2048,128]{3,1,2,0:T(2,128)(2,1)} %scatter_fusion.3, f32[4,2,2048]{2,1,0:T(2,128)S(1)} %copy-done.24, bf16[4,2,2048,128]{3,2,1,0:T(8,128)(2,1)} %param.21, f32[4,2,32,2048]{3,2,1,0:T(8,128)} %get-tuple-element.58, ...), kind=kOutput, calls=%fused_computation.64 | convolution fusion | flops 144179200 | bytes 10699776 | tf_op jit(solution)/shard_map/bhqk,bhkd->bhqd/dot_general | solution.py:26
  140.8 1.9 convert_reduce_fusion.1
  142.7 0.3 copy-done.5
  143.0 1.0 fusion.63
  144.2 0.2 convolution_bitcast_fusion.7
  145.6 0.7 pad_maximum_fusion.2
  146.3 0.7 pad_maximum_fusion.4
  147.1 0.7 all_to_all.101
  147.8 3.2 all-to-all-start.1
  151.0 0.7 all_to_all.109
  151.7 5.7 %all-to-all-done.1 = f32[1,8,64]{2,0,1:T(1,128)S(1)} async-done(((f32[1,8,64]{2,0,1:T(1,128)}), f32[1,8,64]{2,0,1:T(1,128)S(1)}, u32[]{:S(2)}, u32[]{:S(2)}) %all-to-all-start.1) | async-done | bytes 2080 | tf_op jit(solution)/shard_map/all_to_all | solution.py:63
  157.4 3.3 all-to-all-start.4
  161.0 0.7 all_to_all.112
  161.8 0.7 all_to_all.120
  162.5 0.7 all_to_all.117
  163.4 3.8 %all-to-all-done.4 = f32[1,8,64]{2,0,1:T(1,128)S(1)} async-done(((f32[1,8,64]{2,0,1:T(1,128)}), f32[1,8,64]{2,0,1:T(1,128)S(1)}, u32[]{:S(2)}, u32[]{:S(2)}) %all-to-all-start.4) | async-done | bytes 2080 | tf_op jit(solution)/shard_map/all_to_all | solution.py:63
  167.2 3.3 all-to-all-start.5
  170.5 6.4 %all-to-all-done.5 = f32[1,8,64]{2,0,1:T(1,128)S(1)} async-done(((f32[1,8,64]{2,0,1:T(1,128)}), f32[1,8,64]{2,0,1:T(1,128)S(1)}, u32[]{:S(2)}, u32[]{:S(2)}) %all-to-all-start.5) | async-done | bytes 2080 | tf_op jit(solution)/shard_map/all_to_all | solution.py:64
  176.9 3.3 all-to-all-start.8
  180.3 6.3 %all-to-all-done.8 = f32[1,8,64]{2,0,1:T(1,128)S(1)} async-done(((f32[1,8,64]{2,0,1:T(1,128)}), f32[1,8,64]{2,0,1:T(1,128)S(1)}, u32[]{:S(2)}, u32[]{:S(2)}) %all-to-all-start.8) | async-done | bytes 2080 | tf_op jit(solution)/shard_map/all_to_all | solution.py:64
  186.6 3.2 all-to-all-start.7
  189.9 6.3 %all-to-all-done.7 = f32[1,8,64]{2,0,1:T(1,128)S(1)} async-done(((f32[1,8,64]{2,0,1:T(1,128)}), f32[1,8,64]{2,0,1:T(1,128)S(1)}, u32[]{:S(2)}, u32[]{:S(2)}) %all-to-all-start.7) | async-done | bytes 2080 | tf_op jit(solution)/shard_map/all_to_all | solution.py:63
  196.2 3.4 %all-to-all-start = ((f32[1,512,128]{2,0,1:T(1,128)}), f32[1,512,128]{2,0,1:T(1,128)S(1)}, u32[]{:S(2)}, u32[]{:S(2)}) async-start(f32[1,512,128]{2,0,1:T(1,128)} %bitcast.6), calls=%async_computation | async-start | bytes 524288 | tf_op jit(solution)/shard_map/all_to_all | solution.py:65
  199.9 7.9 %all-to-all-done = f32[1,512,128]{2,0,1:T(1,128)S(1)} async-done(((f32[1,512,128]{2,0,1:T(1,128)}), f32[1,512,128]{2,0,1:T(1,128)S(1)}, u32[]{:S(2)}, u32[]{:S(2)}) %all-to-all-start) | async-done | bytes 262176 | tf_op jit(solution)/shard_map/all_to_all | solution.py:65
  207.8 3.4 %all-to-all-start.3 = ((f32[1,512,128]{2,0,1:T(1,128)}), f32[1,512,128]{2,0,1:T(1,128)S(1)}, u32[]{:S(2)}, u32[]{:S(2)}) async-start(f32[1,512,128]{2,0,1:T(1,128)} %bitcast.43), calls=%async_computation.3 | async-start | bytes 524288 | tf_op jit(solution)/shard_map/all_to_all | solution.py:65
  211.5 32.1 %all_gather.9 = bf16[512,128]{1,0:T(8,128)(2,1)S(1)} all-gather(bf16[64,128]{1,0:T(8,128)(2,1)S(1)} %divide_convert_fusion.2), channel_id=1, replica_groups=mesh['seq'=8,'tp'=4] {'seq'}, dimensions={0}, use_global_device_ids=true | all-gather | bytes 147456 | tf_op jit(solution)/shard_map/all_gather | solution.py:83
  243.7 3.0 fusion.171
  246.7 4.5 %all-to-all-start.6 = ((f32[1,512,128]{2,0,1:T(1,128)}), f32[1,512,128]{2,0,1:T(1,128)S(1)}, u32[]{:S(2)}, u32[]{:S(2)}) async-start(f32[1,512,128]{2,0,1:T(1,128)} %bitcast.80), calls=%async_computation.6 | async-start | bytes 524288 | tf_op jit(solution)/shard_map/all_to_all | solution.py:65
  251.5 32.0 %all_gather.10 = bf16[512,128]{1,0:T(8,128)(2,1)S(1)} all-gather(bf16[64,128]{1,0:T(8,128)(2,1)S(1)} %divide_convert_fusion.1), channel_id=1, replica_groups=mesh['seq'=8,'tp'=4] {'seq'}, dimensions={0}, use_global_device_ids=true | all-gather | bytes 147456 | tf_op jit(solution)/shard_map/all_gather | solution.py:83
  283.5 3.0 fusion.172
  286.8 30.5 %all_gather.11 = bf16[512,128]{1,0:T(8,128)(2,1)S(1)} all-gather(bf16[64,128]{1,0:T(8,128)(2,1)S(1)} %divide_convert_fusion), channel_id=1, replica_groups=mesh['seq'=8,'tp'=4] {'seq'}, dimensions={0}, use_global_device_ids=true | all-gather | bytes 147456 | tf_op jit(solution)/shard_map/all_gather | solution.py:83
  317.4 3.0 fusion.173
  320.4 14.8 %all-reduce.3 = (bf16[32,1024]{1,0:T(8,128)(2,1)S(1)}, bf16[32,1024]{1,0:T(8,128)(2,1)S(1)}, bf16[32,1024]{1,0:T(8,128)(2,1)S(1)}) all-reduce(f32[32,1024]{1,0:T(8,128)S(1)} %fusion.173, f32[32,1024]{1,0:T(8,128)S(1)} %fusion.172, f32[32,1024]{1,0:T(8,128)S(1)} %fusion.171), channel_id=1, replica_groups=mesh['seq'=8,'tp'=4] {'tp'}, use_global_device_ids=true, to_apply=%region_42.43 | all-reduce | flops 98304 | bytes 589824 | tf_op jit(solution)/shard_map/psum | solution.py:136
  335.2 0.7 pad_maximum_fusion.6
  (125 shorter events, 4.9 us)
Async XLA Ops:
  0.0 4.6 %copy-start.7 = (bf16[4,2,2048,128]{3,2,1,0:T(8,128)(2,1)S(1)}, bf16[4,2,2048,128]{3,2,1,0:T(8,128)(2,1)}, u32[]{:S(2)}) copy-start(bf16[4,2,2048,128]{3,2,1,0:T(8,128)(2,1)} %param.19) | copy-start | bytes 12582916
  4.6 2.0 copy-start.17
  4.6 2.0 copy-start.18
  4.6 2.1 copy-start.16
  6.7 4.0 %copy-start.2 = (bf16[4,2,2048,128]{3,2,1,0:T(8,128)(2,1)S(1)}, bf16[4,2,2048,128]{3,2,1,0:T(8,128)(2,1)}, u32[]{:S(2)}) copy-start(bf16[4,2,2048,128]{3,2,1,0:T(8,128)(2,1)} %copy.174) | copy-start | bytes 12582916
  6.7 4.0 %copy-start.22 = (f32[4,2,2048]{2,1,0:T(2,128)S(1)}, f32[4,2,2048]{2,1,0:T(2,128)}, u32[]{:S(2)}) copy-start(f32[4,2,2048]{2,1,0:T(2,128)} %param.22) | copy-start | bytes 196612
  16.6 1.3 copy-start.8
  16.6 9.3 %copy-start.14 = (bf16[1024,2,256]{2,1,0:T(2,128)(2,1)S(1)}, bf16[1024,2,256]{2,1,0:T(2,128)(2,1)}, u32[]{:S(2)}) copy-start(bf16[1024,2,256]{2,1,0:T(2,128)(2,1)} %param.14) | copy-start | bytes 3145732
  17.9 8.2 %copy-start.15 = (bf16[3,16,1024]{2,1,0:T(8,128)(2,1)S(1)}, bf16[3,16,1024]{2,1,0:T(8,128)(2,1)}, u32[]{:S(2)}) copy-start(bf16[3,16,1024]{2,1,0:T(8,128)(2,1)} %param.13) | copy-start | bytes 294916
  18.6 129.2 %all-to-all-start.2 = ((f32[1,8,64]{2,0,1:T(1,128)}), f32[1,8,64]{2,0,1:T(1,128)S(1)}, u32[]{:S(2)}, u32[]{:S(2)}) async-start(f32[1,8,64]{2,0,1:T(1,128)} %all_to_all.104), calls=%async_computation.2 | async-start | bytes 8192 | tf_op jit(solution)/shard_map/all_to_all | solution.py:64
  26.1 39.5 %copy-start.21 = (bf16[3,4,2,32,128]{4,3,2,1,0:T(8,128)(2,1)S(1)}, bf16[3,4,2,32,128]{4,3,2,1,0:T(8,128)(2,1)}, u32[]{:S(2)}) copy-start(bf16[3,4,2,32,128]{4,3,2,1,0:T(8,128)(2,1)} %param.16) | copy-start | bytes 589828
  69.3 13.3 %copy-start.23 = (f32[4,2,2048]{2,1,0:T(2,128)S(1)}, f32[4,2,2048]{2,1,0:T(2,128)}, u32[]{:S(2)}) copy-start(f32[4,2,2048]{2,1,0:T(2,128)} %param.22) | copy-start | bytes 196612
  82.6 8.5 %copy-start.6 = (bf16[4,2,2048,128]{3,1,2,0:T(2,128)(2,1)S(1)}, bf16[4,2,2048,128]{3,1,2,0:T(2,128)(2,1)}, u32[]{:S(2)}) copy-start(bf16[4,2,2048,128]{3,1,2,0:T(2,128)(2,1)} %scatter_fusion.2) | copy-start | bytes 12582916
  82.6 11.4 %copy-start.19 = (bf16[4,2,2048,128]{3,2,1,0:T(8,128)(2,1)S(1)}, bf16[4,2,2048,128]{3,2,1,0:T(8,128)(2,1)}, u32[]{:S(2)}) copy-start(bf16[4,2,2048,128]{3,2,1,0:T(8,128)(2,1)} %param.20) | copy-start | bytes 12582916
  91.1 2.9 copy-start.3
  100.2 2.8 copy-start
  103.1 1.6 copy-start.9
  103.1 2.8 copy-start.20
  103.1 2.8 copy-start.24
  113.4 10.6 %copy-start.1 = (bf16[4,2,2048,128]{3,2,1,0:T(8,128)(2,1)S(1)}, bf16[4,2,2048,128]{3,2,1,0:T(8,128)(2,1)}, u32[]{:S(2)}) copy-start(bf16[4,2,2048,128]{3,2,1,0:T(8,128)(2,1)} %scatter_fusion.1) | copy-start | bytes 12582916
  113.4 10.6 %copy-start.12 = (f32[4,2,32,2048]{3,2,1,0:T(8,128)S(1)}, f32[4,2,32,2048]{3,2,1,0:T(8,128)}, u32[]{:S(2)}) copy-start(f32[4,2,32,2048]{3,2,1,0:T(8,128)} %get-tuple-element.70) | copy-start | bytes 6291460
  124.0 6.0 %copy-start.4 = (f32[4,2,32,2048]{3,2,1,0:T(8,128)S(1)}, f32[4,2,32,2048]{3,2,1,0:T(8,128)}, u32[]{:S(2)}) copy-start(f32[4,2,32,2048]{3,2,1,0:T(8,128)} %get-tuple-element.68) | copy-start | bytes 6291460
  133.6 7.2 %copy-start.10 = (f32[4,2,32,2048]{3,2,1,0:T(8,128)S(1)}, f32[4,2,32,2048]{3,2,1,0:T(8,128)}, u32[]{:S(2)}) copy-start(f32[4,2,32,2048]{3,2,1,0:T(8,128)} %get-tuple-element.56) | copy-start | bytes 6291460
  133.6 7.2 %copy-start.11 = (f32[4,2,32,2048]{3,2,1,0:T(8,128)S(1)}, f32[4,2,32,2048]{3,2,1,0:T(8,128)}, u32[]{:S(2)}) copy-start(f32[4,2,32,2048]{3,2,1,0:T(8,128)} %get-tuple-element.58) | copy-start | bytes 6291460
  133.6 7.2 %copy-start.13 = (f32[4,2,32,2048]{3,2,1,0:T(8,128)S(1)}, f32[4,2,32,2048]{3,2,1,0:T(8,128)}, u32[]{:S(2)}) copy-start(f32[4,2,32,2048]{3,2,1,0:T(8,128)} %get-tuple-element.70) | copy-start | bytes 6291460
  140.8 2.2 copy-start.5
  147.8 9.7 %all-to-all-start.1 = ((f32[1,8,64]{2,0,1:T(1,128)}), f32[1,8,64]{2,0,1:T(1,128)S(1)}, u32[]{:S(2)}, u32[]{:S(2)}) async-start(f32[1,8,64]{2,0,1:T(1,128)} %all_to_all.101), calls=%async_computation.1 | async-start | bytes 8192 | tf_op jit(solution)/shard_map/all_to_all | solution.py:63
  157.4 9.8 %all-to-all-start.4 = ((f32[1,8,64]{2,0,1:T(1,128)}), f32[1,8,64]{2,0,1:T(1,128)S(1)}, u32[]{:S(2)}, u32[]{:S(2)}) async-start(f32[1,8,64]{2,0,1:T(1,128)} %all_to_all.109), calls=%async_computation.4 | async-start | bytes 8192 | tf_op jit(solution)/shard_map/all_to_all | solution.py:63
  167.2 9.7 %all-to-all-start.5 = ((f32[1,8,64]{2,0,1:T(1,128)}), f32[1,8,64]{2,0,1:T(1,128)S(1)}, u32[]{:S(2)}, u32[]{:S(2)}) async-start(f32[1,8,64]{2,0,1:T(1,128)} %all_to_all.112), calls=%async_computation.5 | async-start | bytes 8192 | tf_op jit(solution)/shard_map/all_to_all | solution.py:64
  176.9 9.7 %all-to-all-start.8 = ((f32[1,8,64]{2,0,1:T(1,128)}), f32[1,8,64]{2,0,1:T(1,128)S(1)}, u32[]{:S(2)}, u32[]{:S(2)}) async-start(f32[1,8,64]{2,0,1:T(1,128)} %all_to_all.120), calls=%async_computation.8 | async-start | bytes 8192 | tf_op jit(solution)/shard_map/all_to_all | solution.py:64
  186.6 9.7 %all-to-all-start.7 = ((f32[1,8,64]{2,0,1:T(1,128)}), f32[1,8,64]{2,0,1:T(1,128)S(1)}, u32[]{:S(2)}, u32[]{:S(2)}) async-start(f32[1,8,64]{2,0,1:T(1,128)} %all_to_all.117), calls=%async_computation.7 | async-start | bytes 8192 | tf_op jit(solution)/shard_map/all_to_all | solution.py:63
  196.2 11.6 %all-to-all-start = ((f32[1,512,128]{2,0,1:T(1,128)}), f32[1,512,128]{2,0,1:T(1,128)S(1)}, u32[]{:S(2)}, u32[]{:S(2)}) async-start(f32[1,512,128]{2,0,1:T(1,128)} %bitcast.6), calls=%async_computation | async-start | bytes 524288 | tf_op jit(solution)/shard_map/all_to_all | solution.py:65
  207.8 38.8 %all-to-all-start.3 = ((f32[1,512,128]{2,0,1:T(1,128)}), f32[1,512,128]{2,0,1:T(1,128)S(1)}, u32[]{:S(2)}, u32[]{:S(2)}) async-start(f32[1,512,128]{2,0,1:T(1,128)} %bitcast.43), calls=%async_computation.3 | async-start | bytes 524288 | tf_op jit(solution)/shard_map/all_to_all | solution.py:65
  246.7 39.8 %all-to-all-start.6 = ((f32[1,512,128]{2,0,1:T(1,128)}), f32[1,512,128]{2,0,1:T(1,128)S(1)}, u32[]{:S(2)}, u32[]{:S(2)}) async-start(f32[1,512,128]{2,0,1:T(1,128)} %bitcast.80), calls=%async_computation.6 | async-start | bytes 524288 | tf_op jit(solution)/shard_map/all_to_all | solution.py:65
where the time goes:
time: 337 us; the launch traced here: 336 us
  blocking collectives  148 us (44%)
  matrix products  62.7 us (19%)
  local copies, waits for them, and re-layouts  45.8 us (14%)
  waiting for transfers between devices  36.6 us (11%)
  starting transfers between devices  35 us (10%)
  other arithmetic  7.3 us (2%)
    all_gather x3, blocking collectives, spread_merge(): gathered = lax.all_gather(merged, 'seq', axis=0, tiled=True)  94.5 us
    psum x1, blocking collectives, per_device(): lax.psum(partial_kv, 'seq').astype(jnp.bfloat16)  38.5 us
    dot_general x12, matrix products, attend(): jnp.einsum('bhqd,bhkd->bhqk', queries, keys, preferred_element_type=jnp.f...  31.3 us
    dot_general x12, matrix products, attend(): jnp.einsum('bhqk,bhkd->bhqd', weights, values, preferred_element_type=jnp...  21.6 us
    all_to_all x3, waiting for transfers between devices, spread_merge(): lax.all_to_all(maxima, 'seq', split_axis=1, concat_axis=0, tiled=True)  15.9 us
    scatter x3, local copies, waits for them, and re-layouts, per_device(): values_cache.at[batch_rows, :, targets, :]  15.7 us
    scatter x3, local copies, waits for them, and re-layouts, per_device(): keys_cache.at[batch_rows, :, targets, :]  15.6 us
    psum x1, blocking collectives, per_device(): summed = lax.psum(projected, 'tp')  14.8 us
  transfers between devices with their start and end apart: 9, of which 6 were waited for; matrix products, arithmetic and copies ran while one was open for 26% of the time, Pallas kernels for 0%

commit v1 on v0

--- a/solution.py
+++ b/solution.py
@@ -61,7 +61,15 @@
     maxima, totals, weighted = stacked_rows(draft_part, verify_part)
     maxima, totals, weighted = (
         lax.all_to_all(maxima, "seq", split_axis=1, concat_axis=0, tiled=True),
-        lax.all_to_all(totals, "seq", split_axis=1, concat_axis=0, tiled=True),
+        jnp.concatenate(
+            lax.all_to_all(
+                jnp.stack(jnp.split(totals, lax.axis_size("seq"), axis=1)),
+                "seq",
+                split_axis=0,
+                concat_axis=0,
+            ),
+            axis=0,
+        ),
         lax.all_to_all(weighted, "seq", split_axis=1, concat_axis=0, tiled=True),
     )
     highest = jnp.max(maxima, axis=0)

time: 337 us -> 351 us (1.042)
  local copies, waits for them, and re-layouts: 45.8 us -> 58 us
    unnamed x53 -> x74, local copies, waits for them, and re-layouts: 9.41 us -> 21.5 us
  transfers between devices with their start and end apart: 9 -> 9, of which waited for: 6 -> 6; matrix products, arithmetic and copies ran while one was open for 26% -> 28% of each run, Pallas kernels for 0% -> 0%
where the time goes in v1:
time: 351 us; the launch traced here: 350 us
  blocking collectives  148 us (42%)
  matrix products  62.8 us (18%)
  local copies, waits for them, and re-layouts  58 us (17%)
  waiting for transfers between devices  38 us (11%)
  starting transfers between devices  35.1 us (10%)
  other arithmetic  7.3 us (2%)
    all_gather x3, blocking collectives, spread_merge(): gathered = lax.all_gather(merged, 'seq', axis=0, tiled=True)  94.6 us
    psum x1, blocking collectives, per_device(): lax.psum(partial_kv, 'seq').astype(jnp.bfloat16)  38.5 us
    dot_general x12, matrix products, attend(): jnp.einsum('bhqd,bhkd->bhqk', queries, keys, preferred_element_type=jnp.f...  31.4 us
    dot_general x12, matrix products, attend(): jnp.einsum('bhqk,bhkd->bhqd', weights, values, preferred_element_type=jnp...  21.6 us
    unnamed x74, local copies, waits for them, and re-layouts  21.5 us
    all_to_all x3, waiting for transfers between devices, spread_merge(): lax.all_to_all(maxima, 'seq', split_axis=1, concat_axis=0, tiled=True)  17.3 us
    scatter x3, local copies, waits for them, and re-layouts, per_device(): values_cache.at[batch_rows, :, targets, :]  15.7 us
    scatter x3, local copies, waits for them, and re-layouts, per_device(): keys_cache.at[batch_rows, :, targets, :]  15.5 us
  transfers between devices with their start and end apart: 9, of which 6 were waited for; matrix products, arithmetic and copies ran while one was open for 28% of the time, Pallas kernels for 0%

profile of v1, /device:TPU:0, one launch (start us, length us, event | category | flops | bytes accessed | tf_op | source)
XLA Modules:
  0.0 349.7 jit_solution(16772266583895240744)
XLA Ops:
  0.0 4.6 %copy.195 = bf16[4,2,2048,128]{3,2,1,0:T(8,128)(2,1)} copy(bf16[4,2,2048,128]{3,2,1,0:T(8,128)(2,1)} %param.18) | data formatting | bytes 8388608
  4.6 1.9 copy.196
  6.7 3.9 %fusion.169 = (f32[4,2,32]{2,1,0:T(2,128)S(1)}, f32[4,2,32,2048]{3,2,1,0:T(8,128)S(1)}) fusion(bf16[4,2,2048,128]{3,2,1,0:T(8,128)(2,1)} %copy.195, bf16[3,4,2,32,128]{4,3,2,1,0:T(8,128)(2,1)S(1)} %copy-done.16, pred[4,2048]{1,0:T(4,128)(4,1)S(1)} %get-tuple-element.48), kind=kOutput, calls=%fused_computation.290 | convolution fusion | flops 135790336 | bytes 6366208 | tf_op jit(solution)/shard_map/bhqd,bhkd->bhqk/dot_general | solution.py:19
  10.7 5.9 %fusion.170 = (f32[4,2,32]{2,1,0:T(2,128)S(1)}, f32[4,2,32,2048]{3,2,1,0:T(8,128)S(1)}) fusion(bf16[3,4,2,32,128]{4,3,2,1,0:T(8,128)(2,1)} %param.16, bf16[4,2,2048,128]{3,2,1,0:T(8,128)(2,1)S(1)} %copy-done.2, pred[4,2048]{1,0:T(4,128)(4,1)S(1)} %get-tuple-element.48, f32[4,2,2048]{2,1,0:T(2,128)S(1)} %copy-done.22, bf16[4,2,2048,128]{3,2,1,0:T(8,128)(2,1)} %param.20), kind=kOutput, calls=%fused_computation.291 | convolution fusion | flops 144178944 | bytes 10634240 | tf_op jit(solution)/shard_map/bhqd,bhkd->bhqk/dot_general | solution.py:19
  16.6 0.9 convert_reduce_fusion.5
  18.6 0.6 constant_dynamic-update-slice_fusion.6
  19.8 0.6 constant_dynamic-update-slice_fusion.4
  20.9 0.7 constant_dynamic-update-slice_fusion.2
  22.2 0.6 constant_dynamic-update-slice_fusion
  22.8 7.3 %all-to-all-start.2 = ((f32[8,1,64]{2,1,0:T(1,128)}), f32[8,1,64]{2,1,0:T(1,128)S(1)}, u32[]{:S(2)}, u32[]{:S(2)}) async-start(f32[8,1,64]{2,1,0:T(1,128)} %constant_dynamic-update-slice_fusion), calls=%async_computation.2 | async-start | bytes 8192 | tf_op jit(solution)/shard_map/all_to_all | solution.py:65
  31.1 38.5 %all-reduce = (bf16[16,512]{1,0:T(8,128)(2,1)S(1)}, bf16[16,512]{1,0:T(8,128)(2,1)S(1)}, bf16[16,512]{1,0:T(8,128)(2,1)S(1)}) all-reduce(f32[16,512]{1,0:T(8,128)S(1)} %fusion.111, f32[16,512]{1,0:T(8,128)S(1)} %fusion.115, f32[16,512]{1,0:T(8,128)S(1)} %fusion.113), channel_id=1, replica_groups=mesh['seq'=8,'tp'=4] {'seq'}, use_global_device_ids=true, to_apply=%region_34.35 | all-reduce | flops 24576 | bytes 147456 | tf_op jit(solution)/shard_map/psum | solution.py:127
  71.0 2.5 scatter_fusion
  73.5 10.5 %copy.76 = bf16[4,2,2048,128]{3,1,2,0:T(2,128)(2,1)} copy(bf16[4,2,2048,128]{3,2,1,0:T(8,128)(2,1)} %scatter_fusion) | data formatting | bytes 8388608 | tf_op jit(solution)/shard_map/scatter | solution.py:151
  84.2 2.6 scatter_fusion.2
  86.7 8.5 %fusion.162 = (f32[4,2,32]{2,1,0:T(2,128)S(1)}, f32[4,2,32,2048]{3,2,1,0:T(8,128)}) fusion(bf16[3,4,2,32,128]{4,3,2,1,0:T(8,128)(2,1)S(1)} %copy-done.21, pred[4,2048]{1,0:T(4,128)(4,1)S(1)} %get-tuple-element.48, bf16[4,2,2048,128]{3,1,2,0:T(2,128)(2,1)} %scatter_fusion.2, f32[4,2,2048]{2,1,0:T(2,128)S(1)} %copy-done.23, ...), kind=kOutput, calls=%fused_computation.283 | convolution fusion | flops 144178944 | bytes 10634240 | tf_op jit(solution)/shard_map/bhqd,bhkd->bhqk/dot_general | solution.py:19
  95.2 2.9 fusion.161
  98.2 6.2 %fusion.168 = (f32[4,2,32]{2,1,0:T(2,128)S(1)}, f32[4,2,32,2048]{3,2,1,0:T(8,128)}) fusion(bf16[3,4,2,32,128]{4,3,2,1,0:T(8,128)(2,1)S(1)} %copy-done.21, bf16[4,2,2048,128]{3,2,1,0:T(8,128)(2,1)S(1)} %copy-done.3, pred[4,2048]{1,0:T(4,128)(4,1)S(1)} %get-tuple-element.48, f32[4,2,2048]{2,1,0:T(2,128)S(1)} %copy-done.23, ...), kind=kOutput, calls=%fused_computation.289 | convolution fusion | flops 144178944 | bytes 10634240 | tf_op jit(solution)/shard_map/bhqd,bhkd->bhqk/dot_general | solution.py:19
  104.4 2.9 fusion.167
  107.3 0.9 convolution_bitcast_fusion.1
  108.2 0.6 copy-done.9
  108.9 1.2 copy-done.20
  110.1 4.2 %fusion.66 = f32[1,4,2,32,128]{4,3,2,1,0:T(8,128)S(1)} fusion(bf16[4,2,2048,128]{3,2,1,0:T(8,128)(2,1)S(1)} %copy-done, pred[4,2048]{1,0:T(4,128)(4,1)S(1)} %get-tuple-element.48, f32[4,2,2048]{2,1,0:T(2,128)S(1)} %copy-done.24, bf16[4,2,2048,128]{3,2,1,0:T(8,128)(2,1)S(1)} %copy-done.20, f32[4,2,32,2048]{3,2,1,0:T(8,128)S(1)} %copy-done.9, ...), kind=kOutput, calls=%fused_computation.62 | convolution fusion | flops 144179200 | bytes 10691584 | tf_op jit(solution)/shard_map/bhqk,bhkd->bhqd/dot_general | solution.py:26
  114.4 0.7 pad_maximum_fusion
  115.1 2.5 scatter_fusion.1
  117.6 10.6 %copy.80 = bf16[4,2,2048,128]{3,1,2,0:T(2,128)(2,1)} copy(bf16[4,2,2048,128]{3,2,1,0:T(8,128)(2,1)} %scatter_fusion.1) | data formatting | bytes 8388608 | tf_op jit(solution)/shard_map/scatter | solution.py:154
  128.2 6.0 %fusion.69 = f32[1,4,2,32,128]{4,3,2,1,0:T(8,128)S(1)} fusion(bf16[4,2,2048,128]{3,2,1,0:T(8,128)(2,1)S(1)} %copy-done.1, pred[4,2048]{1,0:T(4,128)(4,1)S(1)} %get-tuple-element.48, f32[4,2,2048]{2,1,0:T(2,128)S(1)} %copy-done.24, bf16[4,2,2048,128]{3,2,1,0:T(8,128)(2,1)} %param.21, f32[4,2,32,2048]{3,2,1,0:T(8,128)S(1)} %copy-done.12, ...), kind=kOutput, calls=%fused_computation.63 | convolution fusion | flops 144179200 | bytes 10699776 | tf_op jit(solution)/shard_map/bhqk,bhkd->bhqd/dot_general | solution.py:26
  134.3 0.9 convolution_bitcast_fusion
  135.2 2.7 scatter_fusion.3
  137.8 7.2 %fusion.72 = f32[1,4,2,32,128]{4,3,2,1,0:T(8,128)S(1)} fusion(pred[4,2048]{1,0:T(4,128)(4,1)S(1)} %get-tuple-element.48, bf16[4,2,2048,128]{3,1,2,0:T(2,128)(2,1)} %scatter_fusion.3, f32[4,2,2048]{2,1,0:T(2,128)S(1)} %copy-done.24, bf16[4,2,2048,128]{3,2,1,0:T(8,128)(2,1)} %param.21, f32[4,2,32,2048]{3,2,1,0:T(8,128)} %get-tuple-element.58, ...), kind=kOutput, calls=%fused_computation.64 | convolution fusion | flops 144179200 | bytes 10699776 | tf_op jit(solution)/shard_map/bhqk,bhkd->bhqd/dot_general | solution.py:26
  145.1 1.9 convert_reduce_fusion.1
  147.3 1.0 fusion.63
  149.8 0.6 constant_dynamic-update-slice_fusion.15
  150.4 0.6 constant_dynamic-update-slice_fusion.14
  151.6 0.6 constant_dynamic-update-slice_fusion.12
  152.2 0.6 constant_dynamic-update-slice_fusion.11
  154.0 0.6 constant_dynamic-update-slice_fusion.8
  155.2 0.6 constant_dynamic-update-slice_fusion.22
  159.2 0.7 pad_maximum_fusion.2
  159.9 0.7 pad_maximum_fusion.4
  160.7 0.7 all_to_all.74
  161.4 3.3 all-to-all-start.1
  164.7 0.7 all_to_all.80
  165.4 5.7 %all-to-all-done.1 = f32[1,8,64]{2,0,1:T(1,128)S(1)} async-done(((f32[1,8,64]{2,0,1:T(1,128)}), f32[1,8,64]{2,0,1:T(1,128)S(1)}, u32[]{:S(2)}, u32[]{:S(2)}) %all-to-all-start.1) | async-done | bytes 2080 | tf_op jit(solution)/shard_map/all_to_all | solution.py:63
  171.1 3.2 all-to-all-start.4
  174.8 0.7 all_to_all.86
  175.6 5.2 %all-to-all-done.4 = f32[1,8,64]{2,0,1:T(1,128)S(1)} async-done(((f32[1,8,64]{2,0,1:T(1,128)}), f32[1,8,64]{2,0,1:T(1,128)S(1)}, u32[]{:S(2)}, u32[]{:S(2)}) %all-to-all-start.4) | async-done | bytes 2080 | tf_op jit(solution)/shard_map/all_to_all | solution.py:63
  180.8 3.3 all-to-all-start.5
  184.2 6.4 %all-to-all-done.5 = f32[8,1,64]{2,1,0:T(1,128)S(1)} async-done(((f32[8,1,64]{2,1,0:T(1,128)}), f32[8,1,64]{2,1,0:T(1,128)S(1)}, u32[]{:S(2)}, u32[]{:S(2)}) %all-to-all-start.5) | async-done | bytes 2080 | tf_op jit(solution)/shard_map/all_to_all | solution.py:65
  190.6 3.3 all-to-all-start.8
  193.9 6.3 %all-to-all-done.8 = f32[8,1,64]{2,1,0:T(1,128)S(1)} async-done(((f32[8,1,64]{2,1,0:T(1,128)}), f32[8,1,64]{2,1,0:T(1,128)S(1)}, u32[]{:S(2)}, u32[]{:S(2)}) %all-to-all-start.8) | async-done | bytes 2080 | tf_op jit(solution)/shard_map/all_to_all | solution.py:65
  200.3 3.3 all-to-all-start.7
  203.7 6.3 %all-to-all-done.7 = f32[1,8,64]{2,0,1:T(1,128)S(1)} async-done(((f32[1,8,64]{2,0,1:T(1,128)}), f32[1,8,64]{2,0,1:T(1,128)S(1)}, u32[]{:S(2)}, u32[]{:S(2)}) %all-to-all-start.7) | async-done | bytes 2080 | tf_op jit(solution)/shard_map/all_to_all | solution.py:63
  210.0 3.4 all-to-all-start
  213.7 8.0 %all-to-all-done = f32[1,512,128]{2,0,1:T(1,128)S(1)} async-done(((f32[1,512,128]{2,0,1:T(1,128)}), f32[1,512,128]{2,0,1:T(1,128)S(1)}, u32[]{:S(2)}, u32[]{:S(2)}) %all-to-all-start) | async-done | bytes 262176 | tf_op jit(solution)/shard_map/all_to_all | solution.py:73
  221.6 3.4 all-to-all-start.3
  225.3 32.1 %all_gather.9 = bf16[512,128]{1,0:T(8,128)(2,1)S(1)} all-gather(bf16[64,128]{1,0:T(8,128)(2,1)S(1)} %divide_convert_fusion.2), channel_id=1, replica_groups=mesh['seq'=8,'tp'=4] {'seq'}, dimensions={0}, use_global_device_ids=true | all-gather | bytes 147456 | tf_op jit(solution)/shard_map/all_gather | solution.py:91
  257.5 3.0 fusion.171
  260.5 4.5 %all-to-all-start.6 = ((f32[1,512,128]{2,0,1:T(1,128)}), f32[1,512,128]{2,0,1:T(1,128)S(1)}, u32[]{:S(2)}, u32[]{:S(2)}) async-start(f32[1,512,128]{2,0,1:T(1,128)} %bitcast.96), calls=%async_computation.6 | async-start | bytes 524288 | tf_op jit(solution)/shard_map/all_to_all | solution.py:73
  265.2 32.0 %all_gather.10 = bf16[512,128]{1,0:T(8,128)(2,1)S(1)} all-gather(bf16[64,128]{1,0:T(8,128)(2,1)S(1)} %divide_convert_fusion.1), channel_id=1, replica_groups=mesh['seq'=8,'tp'=4] {'seq'}, dimensions={0}, use_global_device_ids=true | all-gather | bytes 147456 | tf_op jit(solution)/shard_map/all_gather | solution.py:91
  297.2 3.0 fusion.172
  300.5 30.5 %all_gather.11 = bf16[512,128]{1,0:T(8,128)(2,1)S(1)} all-gather(bf16[64,128]{1,0:T(8,128)(2,1)S(1)} %divide_convert_fusion), channel_id=1, replica_groups=mesh['seq'=8,'tp'=4] {'seq'}, dimensions={0}, use_global_device_ids=true | all-gather | bytes 147456 | tf_op jit(solution)/shard_map/all_gather | solution.py:91
  331.1 3.0 fusion.173
  334.1 14.8 %all-reduce.3 = (bf16[32,1024]{1,0:T(8,128)(2,1)S(1)}, bf16[32,1024]{1,0:T(8,128)(2,1)S(1)}, bf16[32,1024]{1,0:T(8,128)(2,1)S(1)}) all-reduce(f32[32,1024]{1,0:T(8,128)S(1)} %fusion.173, f32[32,1024]{1,0:T(8,128)S(1)} %fusion.172, f32[32,1024]{1,0:T(8,128)S(1)} %fusion.171), channel_id=1, replica_groups=mesh['seq'=8,'tp'=4] {'tp'}, use_global_device_ids=true, to_apply=%region_42.43 | all-reduce | flops 98304 | bytes 589824 | tf_op jit(solution)/shard_map/psum | solution.py:144
  349.0 0.7 pad_maximum_fusion.6
  (149 shorter events, 14.8 us)
Async XLA Ops:
  0.0 4.6 %copy-start.7 = (bf16[4,2,2048,128]{3,2,1,0:T(8,128)(2,1)S(1)}, bf16[4,2,2048,128]{3,2,1,0:T(8,128)(2,1)}, u32[]{:S(2)}) copy-start(bf16[4,2,2048,128]{3,2,1,0:T(8,128)(2,1)} %param.19) | copy-start | bytes 12582916
  4.6 1.9 copy-start.17
  4.6 1.9 copy-start.18
  4.6 2.1 copy-start.16
  6.7 4.0 %copy-start.2 = (bf16[4,2,2048,128]{3,2,1,0:T(8,128)(2,1)S(1)}, bf16[4,2,2048,128]{3,2,1,0:T(8,128)(2,1)}, u32[]{:S(2)}) copy-start(bf16[4,2,2048,128]{3,2,1,0:T(8,128)(2,1)} %copy.195) | copy-start | bytes 12582916
  6.7 4.0 %copy-start.22 = (f32[4,2,2048]{2,1,0:T(2,128)S(1)}, f32[4,2,2048]{2,1,0:T(2,128)}, u32[]{:S(2)}) copy-start(f32[4,2,2048]{2,1,0:T(2,128)} %param.22) | copy-start | bytes 196612
  16.6 1.4 copy-start.8
  16.6 13.5 %copy-start.14 = (bf16[1024,2,256]{2,1,0:T(2,128)(2,1)S(1)}, bf16[1024,2,256]{2,1,0:T(2,128)(2,1)}, u32[]{:S(2)}) copy-start(bf16[1024,2,256]{2,1,0:T(2,128)(2,1)} %param.14) | copy-start | bytes 3145732
  18.0 12.4 %copy-start.15 = (bf16[3,16,1024]{2,1,0:T(8,128)(2,1)S(1)}, bf16[3,16,1024]{2,1,0:T(8,128)(2,1)}, u32[]{:S(2)}) copy-start(bf16[3,16,1024]{2,1,0:T(8,128)(2,1)} %param.13) | copy-start | bytes 294916
  22.8 138.6 %all-to-all-start.2 = ((f32[8,1,64]{2,1,0:T(1,128)}), f32[8,1,64]{2,1,0:T(1,128)S(1)}, u32[]{:S(2)}, u32[]{:S(2)}) async-start(f32[8,1,64]{2,1,0:T(1,128)} %constant_dynamic-update-slice_fusion), calls=%async_computation.2 | async-start | bytes 8192 | tf_op jit(solution)/shard_map/all_to_all | solution.py:65
  30.3 39.5 %copy-start.21 = (bf16[3,4,2,32,128]{4,3,2,1,0:T(8,128)(2,1)S(1)}, bf16[3,4,2,32,128]{4,3,2,1,0:T(8,128)(2,1)}, u32[]{:S(2)}) copy-start(bf16[3,4,2,32,128]{4,3,2,1,0:T(8,128)(2,1)} %param.16) | copy-start | bytes 589828
  73.5 13.2 %copy-start.23 = (f32[4,2,2048]{2,1,0:T(2,128)S(1)}, f32[4,2,2048]{2,1,0:T(2,128)}, u32[]{:S(2)}) copy-start(f32[4,2,2048]{2,1,0:T(2,128)} %param.22) | copy-start | bytes 196612
  86.7 8.5 %copy-start.6 = (bf16[4,2,2048,128]{3,1,2,0:T(2,128)(2,1)S(1)}, bf16[4,2,2048,128]{3,1,2,0:T(2,128)(2,1)}, u32[]{:S(2)}) copy-start(bf16[4,2,2048,128]{3,1,2,0:T(2,128)(2,1)} %scatter_fusion.2) | copy-start | bytes 12582916
  86.7 11.4 %copy-start.19 = (bf16[4,2,2048,128]{3,2,1,0:T(8,128)(2,1)S(1)}, bf16[4,2,2048,128]{3,2,1,0:T(8,128)(2,1)}, u32[]{:S(2)}) copy-start(bf16[4,2,2048,128]{3,2,1,0:T(8,128)(2,1)} %param.20) | copy-start | bytes 12582916
  95.2 3.0 copy-start.3
  104.4 2.9 copy-start
  107.3 1.6 copy-start.9
  107.3 2.8 copy-start.20
  107.3 2.8 copy-start.24
  117.6 10.6 %copy-start.1 = (bf16[4,2,2048,128]{3,2,1,0:T(8,128)(2,1)S(1)}, bf16[4,2,2048,128]{3,2,1,0:T(8,128)(2,1)}, u32[]{:S(2)}) copy-start(bf16[4,2,2048,128]{3,2,1,0:T(8,128)(2,1)} %scatter_fusion.1) | copy-start | bytes 12582916
  117.6 10.6 %copy-start.12 = (f32[4,2,32,2048]{3,2,1,0:T(8,128)S(1)}, f32[4,2,32,2048]{3,2,1,0:T(8,128)}, u32[]{:S(2)}) copy-start(f32[4,2,32,2048]{3,2,1,0:T(8,128)} %get-tuple-element.70) | copy-start | bytes 6291460
  128.2 6.0 %copy-start.4 = (f32[4,2,32,2048]{3,2,1,0:T(8,128)S(1)}, f32[4,2,32,2048]{3,2,1,0:T(8,128)}, u32[]{:S(2)}) copy-start(f32[4,2,32,2048]{3,2,1,0:T(8,128)} %get-tuple-element.68) | copy-start | bytes 6291460
  137.8 7.2 %copy-start.10 = (f32[4,2,32,2048]{3,2,1,0:T(8,128)S(1)}, f32[4,2,32,2048]{3,2,1,0:T(8,128)}, u32[]{:S(2)}) copy-start(f32[4,2,32,2048]{3,2,1,0:T(8,128)} %get-tuple-element.56) | copy-start | bytes 6291460
  137.8 7.2 %copy-start.11 = (f32[4,2,32,2048]{3,2,1,0:T(8,128)S(1)}, f32[4,2,32,2048]{3,2,1,0:T(8,128)}, u32[]{:S(2)}) copy-start(f32[4,2,32,2048]{3,2,1,0:T(8,128)} %get-tuple-element.58) | copy-start | bytes 6291460
  137.8 7.2 %copy-start.13 = (f32[4,2,32,2048]{3,2,1,0:T(8,128)S(1)}, f32[4,2,32,2048]{3,2,1,0:T(8,128)}, u32[]{:S(2)}) copy-start(f32[4,2,32,2048]{3,2,1,0:T(8,128)} %get-tuple-element.70) | copy-start | bytes 6291460
  145.1 2.2 copy-start.5
  161.4 9.8 %all-to-all-start.1 = ((f32[1,8,64]{2,0,1:T(1,128)}), f32[1,8,64]{2,0,1:T(1,128)S(1)}, u32[]{:S(2)}, u32[]{:S(2)}) async-start(f32[1,8,64]{2,0,1:T(1,128)} %all_to_all.74), calls=%async_computation.1 | async-start | bytes 8192 | tf_op jit(solution)/shard_map/all_to_all | solution.py:63
  171.1 9.7 %all-to-all-start.4 = ((f32[1,8,64]{2,0,1:T(1,128)}), f32[1,8,64]{2,0,1:T(1,128)S(1)}, u32[]{:S(2)}, u32[]{:S(2)}) async-start(f32[1,8,64]{2,0,1:T(1,128)} %all_to_all.80), calls=%async_computation.4 | async-start | bytes 8192 | tf_op jit(solution)/shard_map/all_to_all | solution.py:63
  180.8 9.8 %all-to-all-start.5 = ((f32[8,1,64]{2,1,0:T(1,128)}), f32[8,1,64]{2,1,0:T(1,128)S(1)}, u32[]{:S(2)}, u32[]{:S(2)}) async-start(f32[8,1,64]{2,1,0:T(1,128)} %constant_dynamic-update-slice_fusion.8), calls=%async_computation.5 | async-start | bytes 8192 | tf_op jit(solution)/shard_map/all_to_all | solution.py:65
  190.6 9.7 %all-to-all-start.8 = ((f32[8,1,64]{2,1,0:T(1,128)}), f32[8,1,64]{2,1,0:T(1,128)S(1)}, u32[]{:S(2)}, u32[]{:S(2)}) async-start(f32[8,1,64]{2,1,0:T(1,128)} %constant_dynamic-update-slice_fusion.16), calls=%async_computation.8 | async-start | bytes 8192 | tf_op jit(solution)/shard_map/all_to_all | solution.py:65
  200.3 9.8 %all-to-all-start.7 = ((f32[1,8,64]{2,0,1:T(1,128)}), f32[1,8,64]{2,0,1:T(1,128)S(1)}, u32[]{:S(2)}, u32[]{:S(2)}) async-start(f32[1,8,64]{2,0,1:T(1,128)} %all_to_all.86), calls=%async_computation.7 | async-start | bytes 8192 | tf_op jit(solution)/shard_map/all_to_all | solution.py:63
  210.0 11.6 %all-to-all-start = ((f32[1,512,128]{2,0,1:T(1,128)}), f32[1,512,128]{2,0,1:T(1,128)S(1)}, u32[]{:S(2)}, u32[]{:S(2)}) async-start(f32[1,512,128]{2,0,1:T(1,128)} %bitcast.6), calls=%async_computation | async-start | bytes 524288 | tf_op jit(solution)/shard_map/all_to_all | solution.py:73
  221.6 38.8 %all-to-all-start.3 = ((f32[1,512,128]{2,0,1:T(1,128)}), f32[1,512,128]{2,0,1:T(1,128)S(1)}, u32[]{:S(2)}, u32[]{:S(2)}) async-start(f32[1,512,128]{2,0,1:T(1,128)} %bitcast.51), calls=%async_computation.3 | async-start | bytes 524288 | tf_op jit(solution)/shard_map/all_to_all | solution.py:73
  260.5 39.8 %all-to-all-start.6 = ((f32[1,512,128]{2,0,1:T(1,128)}), f32[1,512,128]{2,0,1:T(1,128)S(1)}, u32[]{:S(2)}, u32[]{:S(2)}) async-start(f32[1,512,128]{2,0,1:T(1,128)} %bitcast.96), calls=%async_computation.6 | async-start | bytes 524288 | tf_op jit(solution)/shard_map/all_to_all | solution.py:73
